TPU v7x, 32 devices: a whole 2x2x4 slice. The times are simulated.
32 devices in a mesh: dp: 2 (over y), expert: 16 (over z, x, core).
Axes of the slice: x: 2, y: 2, z: 4, core: 2. Of those that a mesh axis runs over, the one named last changes fastest.
Arguments:
- tokens: bfloat16 [512, 2880], P(('dp', 'expert')), may hold values from -6 to 6
- grad_out: bfloat16 [512, 2880], P(('dp', 'expert')), may hold values from -6 to 6
- route_ids: int32 [512, 4], P(('dp', 'expert')), may hold values from 0 to 4, all different within a row; in each aligned block of 16 rows (0 to 15, 16 to 31, ...) at most 16 rows name the same one
- route_prob: float32 [512, 4], P(('dp', 'expert')), may hold values from 0.05 to 1
- device_expert: int32 [16], replicated, may hold values from 0 to 4, as said below
- unit_count: int32 [16], replicated, may hold values from 264 to 480, as said below
- expert_weights: bfloat16 [16, 480, 8640], P('expert'), may hold values from -0.109375 to 0.109375
Outputs:
- grad_tokens: bfloat16 [512, 2880], P(('dp', 'expert'))
- grad_weights: bfloat16 [16, 480, 8640], P('expert', 'dp')
Inputs may be any that keep to these rules, and one draw needn't show every extreme that they name: `route_ids`: each row names 4 different experts; the 16 rows of one device name each expert at most 16 times, and in every draw some device names some expert exactly 16 times. `device_expert`: aligned blocks of 16 indices of expert hold 5 experts, ids rising by one from 5 times the block's number; the indices of one expert are consecutive, 3 or 4 of them; every expert has a group. `unit_count`: the counts of the indices of one expert sum to 1440; rows of expert_weights at or past a slot's count are not part of the model.
All inputs are finite; a program needn't handle non-finite values.
Results may differ from a plain program's by a relative error of at most 0.0058.
Values may be sent and summed in bfloat16 or wider, within the bound.
A program may use at most 128 MiB of HBM per device.

v0:
```python
import functools

import jax
import jax.numpy as jnp
from jax import lax
from jax.experimental import pallas as pl
from jax.experimental.pallas import tpu as pltpu
from jax.sharding import PartitionSpec as P

AXES = ("dp", "expert")


def silu_parts(preact):
    sigma = jax.nn.sigmoid(preact)
    return (preact * sigma, sigma * (1.0 + preact * (1.0 - sigma)))


def unit_work(token_rows, grad_rows, slot_weights, unit_mask):
    width = token_rows.shape[1]
    gate_rows = slot_weights[:, :width]
    up_rows = slot_weights[:, width : 2 * width]
    down_rows = slot_weights[:, 2 * width :]
    contract = (((1,), (1,)), ((), ()))
    gate_pre = lax.dot_general(token_rows, gate_rows, contract, preferred_element_type=jnp.float32)
    up_pre = lax.dot_general(token_rows, up_rows, contract, preferred_element_type=jnp.float32)
    back_grad = lax.dot_general(grad_rows, down_rows, contract, preferred_element_type=jnp.float32)
    active, slope = silu_parts(gate_pre)
    hidden = (active * up_pre * unit_mask).astype(jnp.bfloat16)
    grad_gate = (back_grad * up_pre * slope * unit_mask).astype(jnp.bfloat16)
    grad_up = (back_grad * active * unit_mask).astype(jnp.bfloat16)
    partial_value = jnp.dot(grad_gate, gate_rows, preferred_element_type=jnp.float32) + jnp.dot(
        grad_up, up_rows, preferred_element_type=jnp.float32
    )
    return (partial_value, hidden, grad_gate, grad_up)


def weight_terms(token_rows, grad_rows, hidden, grad_gate, grad_up):
    rows_first = (((0,), (0,)), ((), ()))
    return jnp.concatenate(
        [
            lax.dot_general(grad_gate, token_rows, rows_first, preferred_element_type=jnp.float32),
            lax.dot_general(grad_up, token_rows, rows_first, preferred_element_type=jnp.float32),
            lax.dot_general(hidden, grad_rows, rows_first, preferred_element_type=jnp.float32),
        ],
        axis=1,
    )


def send_back(partial_value):
    return lax.all_to_all(partial_value, "expert", split_axis=0, concat_axis=0, tiled=True)


def routed_shards(tokens, grad_out, route_ids, route_prob, device_expert, unit_count, expert_weights):
    token_count, width = tokens.shape
    top_count = route_ids.shape[1]
    devices = lax.axis_size("expert")
    experts = 5 * devices // 16
    capacity = token_count * top_count * 4 // devices
    flat_ids = route_ids.reshape(-1)
    onehot = (flat_ids[:, None] == jnp.arange(experts, dtype=jnp.int32)[None, :]).astype(jnp.int32)
    rank_of = jnp.sum(onehot * jnp.cumsum(onehot, axis=0), axis=1) - 1
    picked = (flat_ids[None, None, :] == device_expert[:, None, None]) & (
        rank_of[None, None, :] == jnp.arange(capacity, dtype=jnp.int32)[None, :, None]
    )
    picked = picked.astype(jnp.float32).reshape(devices * capacity, token_count * top_count)
    by_token = picked.reshape(devices * capacity, token_count, top_count).sum(axis=2)
    route_scale = jnp.dot(picked, route_prob.reshape(-1), precision=lax.Precision.HIGHEST)
    by_token_low = by_token.astype(jnp.bfloat16)
    sent_rows = jnp.dot(by_token_low, tokens, preferred_element_type=jnp.float32).astype(
        jnp.bfloat16
    )
    sent_grads = (
        route_scale[:, None] * jnp.dot(by_token_low, grad_out, preferred_element_type=jnp.float32)
    ).astype(jnp.bfloat16)
    outgoing = jnp.stack([sent_rows, sent_grads], axis=1).reshape(devices, capacity, 2, width)
    position = lax.axis_index("expert")
    unit_limit = lax.dynamic_index_in_dim(unit_count, position, keepdims=False)
    slot_weights = expert_weights[0]
    slot_units = slot_weights.shape[0]
    unit_mask = (jnp.arange(slot_units, dtype=jnp.int32) < unit_limit).astype(jnp.float32)
    arrived = lax.all_to_all(outgoing, "expert", split_axis=0, concat_axis=0, tiled=True)
    row_pairs = arrived.reshape(-1, 2, width)
    partial_value, hidden, grad_gate, grad_up = unit_work(
        row_pairs[:, 0], row_pairs[:, 1], slot_weights, unit_mask
    )
    leading = (arrived.shape[0], arrived.shape[1])
    returned, all_rows, hidden, grad_gate, grad_up = (
        send_back(partial_value.reshape(leading + (width,))),
        arrived,
        hidden.reshape(leading + (slot_units,)),
        grad_gate.reshape(leading + (slot_units,)),
        grad_up.reshape(leading + (slot_units,)),
    )
    row_pairs = all_rows.reshape(-1, 2, width)
    token_rows = row_pairs[:, 0]
    grad_rows = row_pairs[:, 1]
    hidden = hidden.reshape(-1, slot_units)
    grad_gate = grad_gate.reshape(-1, slot_units)
    grad_up = grad_up.reshape(-1, slot_units)
    term_block = weight_terms(token_rows, grad_rows, hidden, grad_gate, grad_up)
    grad_weights = lax.psum_scatter(term_block, "dp", scatter_dimension=0, tiled=True)
    parts = returned.reshape(devices * capacity, width)
    grad_tokens = lax.dot_general(
        by_token,
        parts,
        (((0,), (0,)), ((), ())),
        precision=lax.Precision.HIGHEST,
        preferred_element_type=jnp.float32,
    )
    return (grad_tokens.astype(jnp.bfloat16), grad_weights.astype(jnp.bfloat16)[None])


MESH = pl.DeviceIdType.MESH
STEP = 256


def dense_kernel(
    nz, half, tok, width, experts,
    x_in, g_in, w_in, ids_ref, prob_ref, expert_ref, limit_ref, gt_out, gw_out,
    xs, gs, dy, w, wu, gate_pre, up_pre, gg, gu, hid, acc, send1, recv1, send2, recv2,
    send3, recv3, send4, recv4, gw,
    local_sem, recv_sem, sz, sx, sy, ss, rs_send, rs_recv,
):
    f32, bf16 = jnp.float32, jnp.bfloat16
    y = lax.axis_index("dp")
    position = lax.axis_index("expert")
    z, x, c = position // 4, (position // 2) % 2, position % 2
    oy, ox, oc = 1 - y, 1 - x, 1 - c

    def place(yy, zz, xx, cc):
        return (yy, zz * 4 + xx * 2 + cc)

    def slot(cc, yy, xx, zz):
        return ((cc * 2 + yy) * 2 + xx) * nz + zz

    def rows(s, count=1):
        return pl.ds(pl.multiple_of(s * tok, tok), count * tok)

    zs = [lax.rem(z + k, nz) for k in range(nz)]
    x_nbr, y_nbr, sib = place(y, z, ox, c), place(oy, z, x, c), place(y, z, x, oc)
    z_nbrs = [place(y, zs[k], x, c) for k in range(1, nz)]
    z_sides = (place(y, lax.rem(z + nz - 1, nz), x, c), place(y, lax.rem(z + 1, nz), x, c))
    has_side = (z > 0, z < nz - 1)

    mine = slot(c, y, x, z)
    first = pl.multiple_of(y * half, 16)
    own_x = pltpu.make_async_copy(x_in, xs.at[rows(mine)], local_sem.at[0])
    load_w = pltpu.make_async_copy(w_in.at[0, pl.ds(first, half)], w, local_sem.at[2])
    for copy in (own_x, load_w):
        copy.start()
    barrier = pltpu.get_barrier_semaphore()
    peers = [x_nbr, y_nbr, sib] + z_nbrs
    for peer in peers:
        pl.semaphore_signal(barrier, inc=1, device_id=peer, device_id_type=MESH)

    spare = gs.shape[1] - width
    lane = lax.broadcasted_iota(jnp.int32, (tok, spare), 1)
    scales = jnp.zeros((tok, spare), f32)
    for k in range(ids_ref.shape[1]):
        scales += jnp.where(ids_ref[:, k : k + 1] == lane % experts, prob_ref[:, k : k + 1], 0.0)
    high = scales.astype(bf16).astype(f32)
    middle = (scales - high).astype(bf16).astype(f32)
    term = lane // experts
    packed = jnp.where(term == 0, high, jnp.where(term == 1, middle, scales - high - middle))
    gs[rows(mine), :width] = g_in[...]
    gs[rows(mine), width:] = jnp.where(term < 3, packed, 0.0).astype(bf16)
    own_x.wait()
    pl.semaphore_wait(barrier, len(peers))

    bufs = (xs, gs)

    def describe(p, s, target, sem):
        return pltpu.make_async_remote_copy(
            src_ref=bufs[p].at[rows(s)], dst_ref=bufs[p].at[rows(s)],
            send_sem=sem, recv_sem=recv_sem.at[p, s], device_id=target, device_id_type=MESH,
        )

    def arrived(p, s):
        describe(p, s, sib, ss.at[p, 0]).wait_recv()

    def along_z(p, zz, side):
        return describe(p, slot(c, y, x, zz), z_sides[side], sz.at[p, side, zz])

    def to_x(p, yy, zz):
        return describe(p, slot(c, yy, x, zz), x_nbr, sx.at[p, (yy if p else 0) * nz + zz])

    def to_y(p, xx, zz):
        return describe(p, slot(c, y, xx, zz), y_nbr, sy.at[p, (0 if p else xx) * nz + zz])

    def to_sib(p, yy, xx, zz):
        return describe(p, slot(c, yy, xx, zz), sib, ss.at[p, (yy * 2 + xx) * nz + zz])

    def spread(p, zz):
        to_x(p, y, zz).start()
        to_y(p, x, zz).start()
        to_sib(p, y, x, zz).start()

    def relay(zz):
        arrived(0, slot(c, y, ox, zz))
        to_y(0, ox, zz).start()
        to_sib(0, y, ox, zz).start()
        arrived(1, slot(c, oy, x, zz))
        to_x(1, oy, zz).start()
        to_sib(1, oy, x, zz).start()

    def at_distance(d, act):
        for side, zz in ((0, z - d), (1, z + d)):
            pl.when((zz >= 0) & (zz < nz))(functools.partial(act, side, zz))

    def from_z(side, zz):
        for p in range(2):
            arrived(p, slot(c, y, x, zz))
            pl.when(has_side[1 - side])(lambda: along_z(p, zz, 1 - side).start())
            spread(p, zz)

    for p in range(2):
        for side in range(2):
            pl.when(has_side[side])(lambda: along_z(p, z, side).start())
        spread(p, z)
    for d in range(1, nz):
        at_distance(d, from_z)
        if d == 1:
            relay(z)
        else:
            at_distance(d - 1, lambda side, zz: relay(zz))
    at_distance(nz - 1, lambda side, zz: relay(zz))
    expert = expert_ref[position]
    lane = lax.broadcasted_iota(jnp.int32, (1, 128), 1) - (128 - spare)
    sel = jnp.where((lane >= 0) & (lane < 3 * experts) & (lane % experts == expert), 1.0, 0.0)
    unit = lax.broadcasted_iota(jnp.int32, (1, half), 1) + y * half
    unit_mask = jnp.where(unit < limit_ref[position], 1.0, 0.0)
    contract = (((1,), (1,)), ((), ()))
    block = 2 * nz * tok
    tail = width // 128 * 128

    def block_rows(cc, yy):
        return pl.ds(pl.multiple_of((cc * 2 + yy) * block, block), block)

    def gate_up(cc, yy):
        r = block_rows(cc, yy)
        gate_pre[r, :] = lax.dot_general(xs[r, :], w[:, :width], contract, preferred_element_type=f32)
        up_pre[r, :] = lax.dot_general(xs[r, :], wu[...], contract, preferred_element_type=f32)

    def backward(cc, yy):
        r = block_rows(cc, yy)
        scale = jnp.sum(gs[r, tail:].astype(f32) * sel, axis=1, keepdims=True)
        dy[r, :] = (scale * gs[r, :width].astype(f32)).astype(bf16)
        b = lax.dot_general(dy[r, :], w[:, 2 * width :], contract, preferred_element_type=f32)
        g, v = gate_pre[r, :], up_pre[r, :]
        live = jnp.broadcast_to(unit_mask, g.shape) > 0.0
        sigma = 1.0 / (1.0 + jnp.exp(-g))
        active = g * sigma
        hid[r, :] = jnp.where(live, active * v, 0.0).astype(bf16)
        gg[r, :] = jnp.where(live, b * v * (sigma * (1.0 + g * (1.0 - sigma))), 0.0).astype(bf16)
        gu[r, :] = jnp.where(live, b * active, 0.0).astype(bf16)

    load_w.wait()
    wu[...] = w[:, width : 2 * width]
    gate_up(c, y)

    def finish(zz):
        for p, yy, xx in ((0, oy, x), (1, y, ox), (0, oy, ox), (1, oy, ox)):
            arrived(p, slot(c, yy, xx, zz))
            to_sib(p, yy, xx, zz).start()

    finish(z)
    for d in range(1, nz - 1):
        at_distance(d, lambda side, zz: finish(zz))
    for k in range(nz):
        for xx in range(2):
            arrived(0, slot(oc, y, xx, k))
    gate_up(oc, y)
    at_distance(nz - 1, lambda side, zz: finish(zz))
    gate_up(c, oy)
    backward(c, y)
    backward(c, oy)
    for k in range(nz):
        for xx in range(2):
            arrived(0, slot(oc, oy, xx, k))
            arrived(1, slot(oc, y, xx, k))
            arrived(1, slot(oc, oy, xx, k))
    gate_up(oc, oy)
    backward(oc, y)
    backward(oc, oy)

    group = nz * tok
    all_rows = 4 * group
    quarter = (width // 128 + 4) // 4 * 128
    strips = [(at, min(at + quarter, width)) for at in range(0, width, quarter)]
    count = len(strips)

    def spans(begin, end):
        return [(at, min(STEP, end - at)) for at in range(begin, end, STEP)]

    def partial(side, at, size):
        r = pl.ds(pl.multiple_of(side * all_rows, all_rows), all_rows)
        return jnp.dot(gg[r, :], w[:, at : at + size], preferred_element_type=f32) + jnp.dot(
            gu[r, :], wu[:, at : at + size], preferred_element_type=f32
        )

    def exchange(index, src, dst, target):
        return pltpu.make_async_remote_copy(
            src_ref=src, dst_ref=dst, send_sem=rs_send.at[index], recv_sem=rs_recv.at[index],
            device_id=target, device_id_type=MESH,
        )

    def grp(yy, xx):
        return pl.ds(pl.multiple_of((yy * 2 + xx) * group, group), group)

    def part(i):
        return pl.ds(pl.multiple_of(i * group, group), group)

    def strip_ref(ref, i):
        begin, end = strips[i]
        return ref.at[:, pl.ds(begin, end - begin)]

    core, second, third, last = [], [], [], []
    for i in range(count):
        even = i % 2 == 0
        core.append(exchange(i, strip_ref(send1, i), strip_ref(recv1, i), sib))
        second.append(exchange(count + i, strip_ref(send2, i), strip_ref(recv2, i), y_nbr if even else x_nbr))
        third.append(exchange(2 * count + i, strip_ref(send3, i), strip_ref(recv3, i), x_nbr if even else y_nbr))

    for i, (begin, end) in enumerate(strips):
        for at, size in spans(begin, end):
            send1[:, at : at + size] = partial(oc, at, size).astype(bf16)
        core[i].start()

    def second_stage(i):
        begin, end = strips[i]
        cols = slice(begin, end)
        for at, size in spans(begin, end):
            acc[:, at : at + size] = partial(c, at, size)
        core[i].wait()
        for j in range(2):
            r = grp(oy, j) if i % 2 == 0 else grp(j, ox)
            send2[j * group : (j + 1) * group, cols] = (acc[r, cols] + recv1[r, cols].astype(f32)).astype(bf16)
        second[i].start()
        for j in range(2):
            r = grp(y, j) if i % 2 == 0 else grp(j, x)
            acc[r, cols] = acc[r, cols] + recv1[r, cols].astype(f32)

    def third_stage(i):
        cols = slice(*strips[i])
        away, stay, r = (ox, x, grp(y, ox)) if i % 2 == 0 else (oy, y, grp(oy, x))
        second[i].wait()
        send3[:, cols] = (acc[r, cols] + recv2[part(away), cols].astype(f32)).astype(bf16)
        third[i].start()
        r = grp(y, x)
        acc[r, cols] = acc[r, cols] + recv2[part(stay), cols].astype(f32)

    def last_stage(i):
        begin, end = strips[i]
        cols = slice(begin, end)
        r = grp(y, x)
        third[i].wait()
        acc[r, cols] = acc[r, cols] + recv3[:, cols].astype(f32)
        send4[:, cols] = acc[r, cols].astype(bf16)
        for k in range(1, nz):
            copy = exchange(
                3 * count + i * (nz - 1) + k - 1,
                send4.at[rows(zs[k]), pl.ds(begin, end - begin)],
                recv4.at[pl.ds((k - 1) * tok, tok), pl.ds(begin, end - begin)],
                z_nbrs[k - 1],
            )
            copy.start()
            last.append(copy)

    def weight_term(left, right, base):
        turned = left[...].T
        for at, size in spans(0, width):
            value = jnp.dot(turned, right[:, at : at + size], preferred_element_type=f32)
            gw[:, base + at : base + at + size] = value.astype(bf16)

    for i in range(count):
        second_stage(i)
    weight_term(gg, xs, 0)
    for i in range(count):
        third_stage(i)
        if i == 1:
            weight_term(gu, xs, width)
    for i in range(count):
        last_stage(i)
    weight_term(hid, dy, 2 * width)
    store_w = pltpu.make_async_copy(gw, gw_out.at[0], local_sem.at[3])
    store_w.start()

    def drain_z(side, zz):
        for p in range(2):
            pl.when(has_side[1 - side])(lambda: along_z(p, zz, 1 - side).wait_send())

    for p in range(2):
        for side in range(2):
            pl.when(has_side[side])(lambda: along_z(p, z, side).wait_send())
    for d in range(1, nz):
        at_distance(d, drain_z)
    for k in range(nz):
        for p in range(2):
            to_x(p, y, k).wait_send()
            to_y(p, x, k).wait_send()
            for yy in range(2):
                for xx in range(2):
                    to_sib(p, yy, xx, k).wait_send()
        to_y(0, ox, k).wait_send()
        to_x(1, oy, k).wait_send()

    total = acc[pl.ds(pl.multiple_of((y * 2 + x) * group + z * tok, tok), tok), :]
    for copy in last:
        copy.wait()
    for k in range(1, nz):
        total = total + recv4[(k - 1) * tok : k * tok, :].astype(f32)
    gt_out[...] = total.astype(bf16)
    store_w.wait()


def dense_shards(tokens, grad_out, route_ids, route_prob, device_expert, unit_count, expert_weights):
    tok, width = tokens.shape
    devices = lax.axis_size("expert")
    nz = devices // 4
    experts = 5 * devices // 16
    half = expert_weights.shape[1] // lax.axis_size("dp")
    spare = 128 - width % 128
    assert 3 * experts <= spare
    padded = width + spare
    n = 2 * devices * tok
    group = nz * tok
    bf16, f32 = jnp.bfloat16, jnp.float32
    vmem = pltpu.VMEM
    dma = pltpu.SemaphoreType.DMA
    any_spec = pl.BlockSpec(memory_space=pl.ANY)
    smem_spec = pl.BlockSpec(memory_space=pltpu.SMEM)
    vmem_spec = pl.BlockSpec(memory_space=pltpu.VMEM)
    return pl.pallas_call(
        functools.partial(dense_kernel, nz, half, tok, width, experts),
        out_shape=(
            jax.ShapeDtypeStruct((tok, width), bf16),
            jax.ShapeDtypeStruct((1, half, 3 * width), bf16),
        ),
        in_specs=[any_spec, vmem_spec, any_spec, vmem_spec, vmem_spec, smem_spec, smem_spec],
        out_specs=(vmem_spec, any_spec),
        scratch_shapes=[
            vmem((n, width), bf16), vmem((n, padded), bf16), vmem((n, width), bf16),
            vmem((half, 3 * width), bf16), vmem((half, width), bf16),
            vmem((n, half), f32), vmem((n, half), f32),
            vmem((n, half), bf16), vmem((n, half), bf16), vmem((n, half), bf16),
            vmem((4 * group, width), f32),
            vmem((4 * group, width), bf16), vmem((4 * group, width), bf16),
            vmem((2 * group, width), bf16), vmem((2 * group, width), bf16),
            vmem((group, width), bf16), vmem((group, width), bf16),
            vmem((group, width), bf16), vmem(((nz - 1) * tok, width), bf16),
            vmem((half, 3 * width), bf16),
            dma((4,)), dma((2, 2 * devices)), dma((2, 2, nz)), dma((2, 2 * nz)), dma((2, 2 * nz)),
            dma((2, 4 * nz)), dma((4 * (nz + 2),)), dma((4 * (nz + 2),)),
        ],
        compiler_params=pltpu.CompilerParams(
            collective_id=0, has_side_effects=True, vmem_limit_bytes=60 * 1024 * 1024
        ),
        name="dense_backward",
    )(tokens, grad_out, expert_weights, route_ids, route_prob, device_expert, unit_count)


def shards(tokens, grad_out, route_ids, *rest):
    token_count = tokens.shape[0]
    capacity = token_count * route_ids.shape[1] * 4 // lax.axis_size("expert")
    form = dense_shards if capacity >= token_count else routed_shards
    return form(tokens, grad_out, route_ids, *rest)


def solution(mesh):
    in_specs = (P(AXES, None),) * 4 + (P(), P(), P("expert", None, None))
    out_specs = (P(AXES, None), P("expert", "dp", None))
    return jax.shard_map(shards, mesh=mesh, in_specs=in_specs, out_specs=out_specs, check_vma=False)
```

profile of v0, /device:TPU:0, one launch (start us, length us, event | category | flops | bytes accessed | tf_op | source)
XLA Modules:
  0.0 73.6 jit_solution(17043879499203916226)
XLA Ops:
  0.6 1.4 %copy.9.ids_ref = s32[16,4]{1,0:T(8,128)} copy(s32[16,4]{0,1:T(4,128)} %param.9) | data formatting | bytes 512 | tf_op args[2]
  2.0 1.4 %copy.10.prob_ref = f32[16,4]{1,0:T(8,128)} copy(f32[16,4]{0,1:T(4,128)} %param.10) | data formatting | bytes 512 | tf_op args[3]
  3.3 64.2 %dense_backward.1 = (bf16[16,2880]{1,0:T(8,128)(2,1)}, bf16[1,240,8640]{2,1,0:T(8,128)(2,1)}) custom-call(bf16[16,2880]{1,0:T(8,128)(2,1)} %x_in.1, bf16[16,2880]{1,0:T(8,128)(2,1)} %g_in.1, bf16[1,480,8640]{2,1,0:T(8,128)(2,1)} %w_in.1, s32[16,4]{1,0:T(8,128)} %copy.9.ids_ref, f32[16,4]{1,0:T(8,128)} %copy.10.prob_ref, s32[16]{0:T(128)} %expert_ref.1, ...), custom_call_target="tpu_custom_call" | custom-call | tf_op jit(solution)/shard_map/dense_backward/pallas_call | solution.py:433
  67.6 1.5 %copy.13 = bf16[16,2880]{1,0:T(8,128)(2,1)} copy(bf16[16,2880]{1,0:T(8,128)(2,1)} %get-tuple-element.4) | data formatting | bytes 184320
  69.1 4.5 %copy.14 = bf16[1,240,8640]{2,1,0:T(8,128)(2,1)} copy(bf16[1,240,8640]{2,1,0:T(8,128)(2,1)} %get-tuple-element.5) | data formatting | bytes 8294400
where the time goes:
time: 73.8 us; the launch traced here: 73.6 us
  Pallas kernels  64.2 us (87%)
  local copies, waits for them, and re-layouts  8.7 us (12%)
    pallas_call x1, Pallas kernels, dense_shards(): pl.pallas_call(functools.partial(dense_kernel, nz, half, tok, width, expe...  64.2 us
    unnamed x4, local copies, waits for them, and re-layouts  8.7 us

commit v1 on v0

v1 whole, which is shorter than its diff:
```python
import functools

import jax
import jax.numpy as jnp
from jax import lax
from jax.experimental import pallas as pl
from jax.experimental.pallas import tpu as pltpu
from jax.sharding import PartitionSpec as P

AXES = ("dp", "expert")


def silu_parts(preact):
    sigma = jax.nn.sigmoid(preact)
    return (preact * sigma, sigma * (1.0 + preact * (1.0 - sigma)))


def unit_work(token_rows, grad_rows, slot_weights, unit_mask):
    width = token_rows.shape[1]
    gate_rows = slot_weights[:, :width]
    up_rows = slot_weights[:, width : 2 * width]
    down_rows = slot_weights[:, 2 * width :]
    contract = (((1,), (1,)), ((), ()))
    gate_pre = lax.dot_general(token_rows, gate_rows, contract, preferred_element_type=jnp.float32)
    up_pre = lax.dot_general(token_rows, up_rows, contract, preferred_element_type=jnp.float32)
    back_grad = lax.dot_general(grad_rows, down_rows, contract, preferred_element_type=jnp.float32)
    active, slope = silu_parts(gate_pre)
    hidden = (active * up_pre * unit_mask).astype(jnp.bfloat16)
    grad_gate = (back_grad * up_pre * slope * unit_mask).astype(jnp.bfloat16)
    grad_up = (back_grad * active * unit_mask).astype(jnp.bfloat16)
    partial_value = jnp.dot(grad_gate, gate_rows, preferred_element_type=jnp.float32) + jnp.dot(
        grad_up, up_rows, preferred_element_type=jnp.float32
    )
    return (partial_value, hidden, grad_gate, grad_up)


def weight_terms(token_rows, grad_rows, hidden, grad_gate, grad_up):
    rows_first = (((0,), (0,)), ((), ()))
    return jnp.concatenate(
        [
            lax.dot_general(grad_gate, token_rows, rows_first, preferred_element_type=jnp.float32),
            lax.dot_general(grad_up, token_rows, rows_first, preferred_element_type=jnp.float32),
            lax.dot_general(hidden, grad_rows, rows_first, preferred_element_type=jnp.float32),
        ],
        axis=1,
    )


def send_back(partial_value):
    return lax.all_to_all(partial_value, "expert", split_axis=0, concat_axis=0, tiled=True)


def routed_shards(tokens, grad_out, route_ids, route_prob, device_expert, unit_count, expert_weights):
    token_count, width = tokens.shape
    top_count = route_ids.shape[1]
    devices = lax.axis_size("expert")
    experts = 5 * devices // 16
    capacity = token_count * top_count * 4 // devices
    flat_ids = route_ids.reshape(-1)
    onehot = (flat_ids[:, None] == jnp.arange(experts, dtype=jnp.int32)[None, :]).astype(jnp.int32)
    rank_of = jnp.sum(onehot * jnp.cumsum(onehot, axis=0), axis=1) - 1
    picked = (flat_ids[None, None, :] == device_expert[:, None, None]) & (
        rank_of[None, None, :] == jnp.arange(capacity, dtype=jnp.int32)[None, :, None]
    )
    picked = picked.astype(jnp.float32).reshape(devices * capacity, token_count * top_count)
    by_token = picked.reshape(devices * capacity, token_count, top_count).sum(axis=2)
    route_scale = jnp.dot(picked, route_prob.reshape(-1), precision=lax.Precision.HIGHEST)
    by_token_low = by_token.astype(jnp.bfloat16)
    sent_rows = jnp.dot(by_token_low, tokens, preferred_element_type=jnp.float32).astype(
        jnp.bfloat16
    )
    sent_grads = (
        route_scale[:, None] * jnp.dot(by_token_low, grad_out, preferred_element_type=jnp.float32)
    ).astype(jnp.bfloat16)
    outgoing = jnp.stack([sent_rows, sent_grads], axis=1).reshape(devices, capacity, 2, width)
    position = lax.axis_index("expert")
    unit_limit = lax.dynamic_index_in_dim(unit_count, position, keepdims=False)
    slot_weights = expert_weights[0]
    slot_units = slot_weights.shape[0]
    unit_mask = (jnp.arange(slot_units, dtype=jnp.int32) < unit_limit).astype(jnp.float32)
    arrived = lax.all_to_all(outgoing, "expert", split_axis=0, concat_axis=0, tiled=True)
    row_pairs = arrived.reshape(-1, 2, width)
    partial_value, hidden, grad_gate, grad_up = unit_work(
        row_pairs[:, 0], row_pairs[:, 1], slot_weights, unit_mask
    )
    leading = (arrived.shape[0], arrived.shape[1])
    returned, all_rows, hidden, grad_gate, grad_up = (
        send_back(partial_value.reshape(leading + (width,))),
        arrived,
        hidden.reshape(leading + (slot_units,)),
        grad_gate.reshape(leading + (slot_units,)),
        grad_up.reshape(leading + (slot_units,)),
    )
    row_pairs = all_rows.reshape(-1, 2, width)
    token_rows = row_pairs[:, 0]
    grad_rows = row_pairs[:, 1]
    hidden = hidden.reshape(-1, slot_units)
    grad_gate = grad_gate.reshape(-1, slot_units)
    grad_up = grad_up.reshape(-1, slot_units)
    term_block = weight_terms(token_rows, grad_rows, hidden, grad_gate, grad_up)
    grad_weights = lax.psum_scatter(term_block, "dp", scatter_dimension=0, tiled=True)
    parts = returned.reshape(devices * capacity, width)
    grad_tokens = lax.dot_general(
        by_token,
        parts,
        (((0,), (0,)), ((), ())),
        precision=lax.Precision.HIGHEST,
        preferred_element_type=jnp.float32,
    )
    return (grad_tokens.astype(jnp.bfloat16), grad_weights.astype(jnp.bfloat16)[None])


MESH = pl.DeviceIdType.MESH
STEP = 256
STRIPS = 4


def split_kernel(
    nz, half, tok, width, experts,
    x_in, g_in, w_in, ids_in, prob_in, expert_ref, limit_ref, gt_out, gw_out,
    xs, gs, own_g, ids, prob, w, wu, gate_pre, up_pre, acts, away_acts, acc,
    send1, recv1, send2, recv2, send3, recv3, gw,
    local_sem, recv_sem, sib_recv, sz, sx, sy, ss, act_send, act_recv, rs_send, rs_recv,
):
    f32, bf16 = jnp.float32, jnp.bfloat16
    y = lax.axis_index("dp")
    position = lax.axis_index("expert")
    z, x, c = position // 4, (position // 2) % 2, position % 2

    def place(yy, zz, xx, cc):
        return (yy, zz * 4 + xx * 2 + cc)

    zs = [lax.rem(z + k, nz) for k in range(nz)]
    x_nbr, y_nbr, sib = place(y, z, 1 - x, c), place(1 - y, z, x, c), place(y, z, x, 1 - c)
    z_nbrs = [place(y, zs[k], x, c) for k in range(1, nz)]
    z_sides = (place(y, lax.rem(z + nz - 1, nz), x, c), place(y, lax.rem(z + 1, nz), x, c))
    has_side = (z > 0, z < nz - 1)
    side_depth = (nz - 1 - z, z)
    barrier = pltpu.get_barrier_semaphore()
    peers = [x_nbr, y_nbr, sib] + z_nbrs
    for peer in peers:
        pl.semaphore_signal(barrier, inc=1, device_id=peer, device_id_type=MESH)

    line = nz * tok
    side_rows = 2 * line
    replica = 2 * side_rows

    def slot(ry, rc, rx, zz):
        return ((ry * 2 + rc) * 2 + rx) * nz + zz

    def rows(s, count=1):
        return pl.ds(pl.multiple_of(s * tok, tok), count * tok)

    mine = slot(0, 0, 0, z)
    own_x = pltpu.make_async_copy(x_in, xs.at[rows(mine)], local_sem.at[0])
    load_g = pltpu.make_async_copy(g_in, own_g, local_sem.at[1])
    load_ids = pltpu.make_async_copy(ids_in, ids, local_sem.at[2])
    load_prob = pltpu.make_async_copy(prob_in, prob, local_sem.at[3])
    for copy in (own_x, load_ids, load_prob, load_g):
        copy.start()
    load_w = []
    for h in range(2):
        first = pl.multiple_of((y if h == 0 else 1 - y) * half, 16)
        load_w.append(pltpu.make_async_copy(w_in.at[0, pl.ds(first, half)], w.at[h], local_sem.at[4 + h]))
        load_w[h].start()

    spare = gs.shape[1] - width
    lane = lax.broadcasted_iota(jnp.int32, (tok, spare), 1)
    diagonal = lax.broadcasted_iota(jnp.int32, (tok, tok), 0) == lax.broadcasted_iota(jnp.int32, (tok, tok), 1)

    def column(row):
        return jnp.sum(jnp.where(diagonal, jnp.broadcast_to(row, (tok, tok)), 0.0), axis=1, keepdims=True)

    load_ids.wait()
    load_prob.wait()
    scales = jnp.zeros((tok, spare), f32)
    which = (lane % experts).astype(f32)
    for k in range(ids.shape[0]):
        named = column(ids[k : k + 1, :].astype(f32))
        scales += jnp.where(named == which, column(prob[k : k + 1, :]), 0.0)
    high = scales.astype(bf16).astype(f32)
    middle = (scales - high).astype(bf16).astype(f32)
    term = lane // experts
    packed = jnp.where(term == 0, high, jnp.where(term == 1, middle, scales - high - middle))
    load_g.wait()
    gs[rows(mine), :width] = own_g[...]
    gs[rows(mine), width:] = jnp.where(term < 3, packed, 0.0).astype(bf16)
    own_x.wait()
    pl.semaphore_wait(barrier, len(peers))

    bufs = (xs, gs)

    def move(p, src, dst, target, send, recv, count=1):
        return pltpu.make_async_remote_copy(
            src_ref=bufs[p].at[rows(src, count)], dst_ref=bufs[p].at[rows(dst, count)],
            send_sem=send, recv_sem=recv, device_id=target, device_id_type=MESH,
        )

    def landing(p, ry, rx, zz):
        return recv_sem.at[p, (ry * 2 + rx) * nz + zz]

    def arrived(p, ry, rx, zz):
        s = slot(ry, 0, rx, zz)
        move(p, s, s, sib, ss.at[p, ry], landing(p, ry, rx, zz)).wait_recv()

    def z_send(p, ry, zz, side):
        s = slot(ry, 0, 0, zz)
        move(p, s, s, z_sides[side], sz.at[(p * 2 + ry) * 2 + side], landing(p, ry, 0, zz)).start()

    def x_send(p, zz):
        move(p, slot(0, 0, 0, zz), slot(0, 0, 1, zz), x_nbr, sx.at[p], landing(p, 0, 1, zz)).start()

    def y_send(p, rx, zz):
        move(p, slot(0, 0, rx, zz), slot(1, 0, rx, zz), y_nbr, sy.at[p], landing(p, 1, rx, zz)).start()

    def sib_send(p, ry, rx, zz):
        move(p, slot(ry, 0, rx, zz), slot(ry, 1, rx, zz), sib, ss.at[p, ry], sib_recv.at[p, ry]).start()

    def sib_arrived(p, ry):
        s = slot(ry, 1, 0, 0)
        move(p, s, s, sib, ss.at[p, ry], sib_recv.at[p, ry], 2 * nz).wait_recv()

    def at_distance(d, act):
        for side, zz in ((0, z - d), (1, z + d)):
            pl.when((zz >= 0) & (zz < nz))(functools.partial(act, side, zz))

    def from_z(side, zz):
        for p in range(2):
            arrived(p, 0, 0, zz)
            pl.when(has_side[1 - side])(lambda: z_send(p, 0, zz, 1 - side))
            x_send(p, zz)
            sib_send(p, 0, 0, zz)

    def relay_x(p, zz):
        arrived(p, 0, 1, zz)
        sib_send(p, 0, 1, zz)
        y_send(p, 1, zz)

    def cross_relay(side, zz):
        def go():
            for p in range(2):
                arrived(p, 1, 0, zz)
                z_send(p, 1, zz, 1 - side)
                sib_send(p, 1, 0, zz)
        pl.when(has_side[1 - side])(go)

    def cross_last(p, side, zz):
        def go():
            arrived(p, 1, 0, zz)
            sib_send(p, 1, 0, zz)
        pl.when(jnp.logical_not(has_side[1 - side]))(go)

    def cross_own(side):
        for p in range(2):
            z_send(p, 1, z, side)

    for p in range(2):
        for side in range(2):
            pl.when(has_side[side])(lambda: z_send(p, 0, z, side))
        x_send(p, z)
        y_send(p, 0, z)
        sib_send(p, 0, 0, z)
    late = nz - 2
    for d in range(1, nz):
        at_distance(d, from_z)
        if d == 1:
            for p in range(2):
                relay_x(p, z)
            for p in range(2):
                arrived(p, 1, 0, z)
                sib_send(p, 1, 0, z)
        elif d - 1 < late:
            for p in range(2):
                at_distance(d - 1, lambda side, zz: relay_x(p, zz))
        for side in range(2):
            ready = side_depth[side] <= 1 if d == 1 else side_depth[side] == d
            pl.when(has_side[side] & ready)(lambda: cross_own(side))

    expert = expert_ref[position]
    lane = lax.broadcasted_iota(jnp.int32, (1, 128), 1) - (128 - spare)
    sel = jnp.where((lane >= 0) & (lane < 3 * experts) & (lane % experts == expert), 1.0, 0.0)
    contract = (((1,), (1,)), ((), ()))
    tail = width // 128 * 128

    for h in range(2):
        load_w[h].wait()
        wu[h] = w[h, :, width : 2 * width]
    at_distance(1, cross_relay)
    for d in range(late, nz):
        at_distance(d, lambda side, zz: relay_x(0, zz))
    sib_arrived(0, 0)
    for h in range(2):
        gate_pre[h] = lax.dot_general(xs[:replica, :], w[h, :, :width], contract, preferred_element_type=f32)
    for d in range(late, nz):
        at_distance(d, lambda side, zz: relay_x(1, zz))
    for d in range(2, nz - 1):
        at_distance(d, cross_relay)
    for h in range(2):
        up_pre[h] = lax.dot_general(xs[:replica, :], wu[h], contract, preferred_element_type=f32)
    sib_arrived(1, 0)

    act_sends = [
        pltpu.make_async_remote_copy(
            src_ref=away_acts.at[k], dst_ref=acts.at[k, pl.ds(replica, replica)],
            send_sem=act_send.at[k], recv_sem=act_recv.at[k], device_id=y_nbr, device_id_type=MESH,
        )
        for k in range(3)
    ]
    scale = jnp.sum(gs[:replica, tail:].astype(f32) * sel, axis=1, keepdims=True)
    for h in (1, 0):
        b = scale * lax.dot_general(
            gs[:replica, :width], w[h, :, 2 * width :], contract, preferred_element_type=f32
        )
        unit = lax.broadcasted_iota(jnp.int32, (1, half), 1) + (y if h == 0 else 1 - y) * half
        unit_mask = jnp.where(unit < limit_ref[position], 1.0, 0.0)
        g, v = gate_pre[h], up_pre[h]
        live = jnp.broadcast_to(unit_mask, g.shape) > 0.0
        sigma = 1.0 / (1.0 + jnp.exp(-g))
        active = g * sigma
        gg = jnp.where(live, b * v * (sigma * (1.0 + g * (1.0 - sigma))), 0.0).astype(bf16)
        gu = jnp.where(live, b * active, 0.0).astype(bf16)
        hid = jnp.where(live, active * v * scale, 0.0).astype(bf16)
        for k, value in enumerate((gg, gu, hid)):
            if h == 0:
                acts[k, :replica, :] = value
            else:
                away_acts[k] = value
                act_sends[k].start()

    quarter = (width // 128 + STRIPS) // STRIPS * 128
    strips = [(at, min(at + quarter, width)) for at in range(0, width, quarter)]
    count = len(strips)

    def spans(begin, end):
        return [(at, min(STEP, end - at)) for at in range(begin, end, STEP)]

    def exchange(stage, i, src, dst, target):
        return pltpu.make_async_remote_copy(
            src_ref=src, dst_ref=dst, send_sem=rs_send.at[stage * count + i],
            recv_sem=rs_recv.at[stage * count + i], device_id=target, device_id_type=MESH,
        )

    def cols(i):
        begin, end = strips[i]
        return pl.ds(begin, end - begin)

    core = [exchange(0, i, send1.at[:, cols(i)], recv1.at[:, cols(i)], sib) for i in range(count)]
    second = [exchange(1, i, send2.at[:, cols(i)], recv2.at[:, cols(i)], x_nbr) for i in range(count)]
    third = [
        exchange(2, i, send3.at[pl.ds(0, (nz - 1) * tok), cols(i)], recv3.at[:, cols(i)], z_nbrs[0])
        for i in range(count)
    ]

    def first_stage(i):
        for at, size in spans(*strips[i]):
            span = slice(at, at + size)
            value = jnp.dot(acts[0, :replica, :], w[0, :, span], preferred_element_type=f32)
            value += jnp.dot(acts[1, :replica, :], wu[0, :, span], preferred_element_type=f32)
            value += jnp.dot(away_acts[0], w[1, :, span], preferred_element_type=f32)
            value += jnp.dot(away_acts[1], wu[1, :, span], preferred_element_type=f32)
            send1[:, span] = value[side_rows:].astype(bf16)
            acc[:, span] = value[:side_rows]
        core[i].start()

    def second_stage(i):
        span = slice(*strips[i])
        core[i].wait()
        send2[:, span] = (acc[line:, span] + recv1[line:, span].astype(f32)).astype(bf16)
        second[i].start()
        acc[:line, span] = acc[:line, span] + recv1[:line, span].astype(f32)

    def third_stage(i):
        span = slice(*strips[i])
        second[i].wait()
        value = acc[:line, span] + recv2[:, span].astype(f32)
        send3[:, span] = value.astype(bf16)
        for k in range(1, nz):
            exchange(
                2, i, send3.at[rows(zs[k]), cols(i)], recv3.at[pl.ds((k - 1) * tok, tok), cols(i)], z_nbrs[k - 1]
            ).start()
        acc[:line, span] = value

    def last_stage(i):
        span = slice(*strips[i])
        third[i].wait()
        total = acc[rows(z), span]
        for k in range(1, nz):
            total = total + recv3[(k - 1) * tok : k * tok, span].astype(f32)
        gt_out[:, span] = total.astype(bf16)

    def weight_term(k, right):
        turned = acts[k].T
        for at, size in spans(0, width):
            value = jnp.dot(turned, right[:, at : at + size], preferred_element_type=f32)
            gw[:, k * width + at : k * width + at + size] = value.astype(bf16)

    for i in range(count):
        first_stage(i)
        if i > 0:
            second_stage(i - 1)
    second_stage(count - 1)
    for p in range(2):
        for d in range(1, nz):
            at_distance(d, functools.partial(cross_last, p))
        for zz in range(nz):
            arrived(p, 1, 1, zz)
            sib_send(p, 1, 1, zz)

    def terms(k):
        if k < 2:
            if k == 0:
                sib_arrived(0, 1)
            act_sends[k].wait_recv()
            weight_term(k, xs)
        elif k == 2:
            sib_arrived(1, 1)
            act_sends[k].wait_recv()
            weight_term(k, gs)

    for i in range(count):
        third_stage(i)
        terms(i)
    for k in range(count, 3):
        terms(k)
    store_w = pltpu.make_async_copy(gw, gw_out.at[0], local_sem.at[6])
    store_w.start()

    def sent(p, ry, side, chunks):
        s = slot(ry, 0, 0, 0)
        move(p, s, s, z_sides[side], sz.at[(p * 2 + ry) * 2 + side], landing(p, ry, 0, 0), chunks).wait_send()

    for p in range(2):
        for ry in range(2):
            for side in range(2):
                for depth in range(nz - 1):
                    pl.when(side_depth[side] == depth)(lambda: sent(p, ry, side, depth + 1))
            move(p, 0, 0, sib, ss.at[p, ry], sib_recv.at[p, ry], 2 * nz).wait_send()
        move(p, 0, 0, x_nbr, sx.at[p], landing(p, 0, 1, 0), nz).wait_send()
        move(p, 0, 0, y_nbr, sy.at[p], landing(p, 1, 0, 0), nz + 1).wait_send()
    for copy in act_sends:
        copy.wait_send()
    for i in range(count):
        last_stage(i)
    store_w.wait()


def dense_shards(tokens, grad_out, route_ids, route_prob, device_expert, unit_count, expert_weights):
    tok, width = tokens.shape
    devices = lax.axis_size("expert")
    nz = devices // 4
    experts = 5 * devices // 16
    half = expert_weights.shape[1] // lax.axis_size("dp")
    spare = 128 - width % 128
    assert 3 * experts <= spare
    padded = width + spare
    replica = devices * tok
    line = nz * tok
    top = route_ids.shape[1]
    bf16, f32 = jnp.bfloat16, jnp.float32
    vmem = pltpu.VMEM
    dma = pltpu.SemaphoreType.DMA
    any_spec = pl.BlockSpec(memory_space=pl.ANY)
    smem_spec = pl.BlockSpec(memory_space=pltpu.SMEM)
    vmem_spec = pl.BlockSpec(memory_space=pltpu.VMEM)
    return pl.pallas_call(
        functools.partial(split_kernel, nz, half, tok, width, experts),
        out_shape=(
            jax.ShapeDtypeStruct((tok, width), bf16),
            jax.ShapeDtypeStruct((1, half, 3 * width), bf16),
        ),
        in_specs=[any_spec] * 5 + [smem_spec] * 2,
        out_specs=(vmem_spec, any_spec),
        scratch_shapes=[
            vmem((2 * replica, width), bf16), vmem((2 * replica, padded), bf16), vmem((tok, width), bf16),
            vmem((top, tok), jnp.int32), vmem((top, tok), f32),
            vmem((2, half, 3 * width), bf16), vmem((2, half, width), bf16),
            vmem((2, replica, half), f32), vmem((2, replica, half), f32),
            vmem((3, 2 * replica, half), bf16), vmem((3, replica, half), bf16),
            vmem((2 * line, width), f32),
            vmem((2 * line, width), bf16), vmem((2 * line, width), bf16),
            vmem((line, width), bf16), vmem((line, width), bf16),
            vmem((line, width), bf16), vmem(((nz - 1) * tok, width), bf16),
            vmem((half, 3 * width), bf16),
            dma((7,)), dma((2, 4 * nz)), dma((2, 2)), dma((8,)), dma((2,)), dma((2,)), dma((2, 2)),
            dma((3,)), dma((3,)), dma((3 * STRIPS,)), dma((3 * STRIPS,)),
        ],
        compiler_params=pltpu.CompilerParams(
            collective_id=0, has_side_effects=True, vmem_limit_bytes=60 * 1024 * 1024
        ),
        name="split_backward",
    )(tokens, grad_out, expert_weights, route_ids.T, route_prob.T, device_expert, unit_count)


def shards(tokens, grad_out, route_ids, *rest):
    token_count = tokens.shape[0]
    capacity = token_count * route_ids.shape[1] * 4 // lax.axis_size("expert")
    form = dense_shards if capacity >= token_count else routed_shards
    return form(tokens, grad_out, route_ids, *rest)


def solution(mesh):
    in_specs = (P(AXES, None),) * 4 + (P(), P(), P("expert", None, None))
    out_specs = (P(AXES, None), P("expert", "dp", None))
    return jax.shard_map(shards, mesh=mesh, in_specs=in_specs, out_specs=out_specs, check_vma=False)
```

time: 73.8 us -> 53.4 us (0.72)
  Pallas kernels: 64.2 us -> 46.6 us
  local copies, waits for them, and re-layouts: 8.7 us -> 5.99 us
    pallas_call x1, Pallas kernels: 64.2 us -> 46.6 us  [dense_shards(): pl.pallas_call(functools.partial(split_kernel, nz, half, tok, width, expe...]
    unnamed x4 -> x2, local copies, waits for them, and re-layouts: 8.7 us -> 5.99 us
where the time goes in v1:
time: 53.4 us; the launch traced here: 53.2 us
  Pallas kernels  46.6 us (87%)
  local copies, waits for them, and re-layouts  5.99 us (11%)
  between operations  0.64 us (1%)
    pallas_call x1, Pallas kernels, dense_shards(): pl.pallas_call(functools.partial(split_kernel, nz, half, tok, width, expe...  46.6 us
    unnamed x2, local copies, waits for them, and re-layouts  5.99 us

profile of v1, /device:TPU:0, one launch (start us, length us, event | category | flops | bytes accessed | tf_op | source)
XLA Modules:
  0.0 53.2 jit_solution(1822821672413666714)
XLA Ops:
  0.6 46.6 %split_backward.1 = (bf16[16,2880]{1,0:T(8,128)(2,1)}, bf16[1,240,8640]{2,1,0:T(8,128)(2,1)}) custom-call(bf16[16,2880]{1,0:T(8,128)(2,1)} %x_in.1, bf16[16,2880]{1,0:T(8,128)(2,1)} %g_in.1, bf16[1,480,8640]{2,1,0:T(8,128)(2,1)} %w_in.1, s32[4,16]{1,0:T(4,128)} %bitcast.2, f32[4,16]{1,0:T(4,128)} %bitcast.3, s32[16]{0:T(128)} %expert_ref.1, s32[16]{0:T(128)} %limit_ref.1), custom_call_target="tpu_custom_call" | custom-call | tf_op jit(solution)/shard_map/split_backward/pallas_call | solution.py:465
  47.2 1.5 %copy.11 = bf16[16,2880]{1,0:T(8,128)(2,1)} copy(bf16[16,2880]{1,0:T(8,128)(2,1)} %get-tuple-element.4) | data formatting | bytes 184320
  48.7 4.5 %copy.12 = bf16[1,240,8640]{2,1,0:T(8,128)(2,1)} copy(bf16[1,240,8640]{2,1,0:T(8,128)(2,1)} %get-tuple-element.5) | data formatting | bytes 8294400

commit v2 on v1

--- a/solution.py
+++ b/solution.py
@@ -113,14 +113,15 @@
 MESH = pl.DeviceIdType.MESH
 STEP = 256
 STRIPS = 4
+VMEM_BYTES = 67043328
 
 
 def split_kernel(
     nz, half, tok, width, experts,
-    x_in, g_in, w_in, ids_in, prob_in, expert_ref, limit_ref, gt_out, gw_out,
+    x_in, g_in, w_in, ids_in, prob_in, expert_ref, limit_ref, gt_out, gw,
     xs, gs, own_g, ids, prob, w, wu, gate_pre, up_pre, acts, away_acts, acc,
-    send1, recv1, send2, recv2, send3, recv3, gw,
-    local_sem, recv_sem, sib_recv, sz, sx, sy, ss, act_send, act_recv, rs_send, rs_recv,
+    send1, recv1, send2, recv2, send3, recv3,
+    local_sem, recv_sem, sib_recv, sz, sx, sy, ss, rs_send, rs_recv,
 ):
     f32, bf16 = jnp.float32, jnp.bfloat16
     y = lax.axis_index("dp")
@@ -229,6 +230,8 @@
             arrived(p, 0, 0, zz)
             pl.when(has_side[1 - side])(lambda: z_send(p, 0, zz, 1 - side))
             x_send(p, zz)
+            if p == 1:
+                y_send(1, 0, zz)
             sib_send(p, 0, 0, zz)
 
     def relay_x(p, zz):
@@ -238,21 +241,16 @@
 
     def cross_relay(side, zz):
         def go():
-            for p in range(2):
-                arrived(p, 1, 0, zz)
-                z_send(p, 1, zz, 1 - side)
-                sib_send(p, 1, 0, zz)
+            arrived(0, 1, 0, zz)
+            z_send(0, 1, zz, 1 - side)
+            sib_send(0, 1, 0, zz)
         pl.when(has_side[1 - side])(go)
 
-    def cross_last(p, side, zz):
+    def cross_last(side, zz):
         def go():
-            arrived(p, 1, 0, zz)
-            sib_send(p, 1, 0, zz)
+            arrived(0, 1, 0, zz)
+            sib_send(0, 1, 0, zz)
         pl.when(jnp.logical_not(has_side[1 - side]))(go)
-
-    def cross_own(side):
-        for p in range(2):
-            z_send(p, 1, z, side)
 
     for p in range(2):
         for side in range(2):
@@ -266,15 +264,14 @@
         if d == 1:
             for p in range(2):
                 relay_x(p, z)
-            for p in range(2):
-                arrived(p, 1, 0, z)
-                sib_send(p, 1, 0, z)
+            arrived(0, 1, 0, z)
+            sib_send(0, 1, 0, z)
         elif d - 1 < late:
             for p in range(2):
                 at_distance(d - 1, lambda side, zz: relay_x(p, zz))
         for side in range(2):
             ready = side_depth[side] <= 1 if d == 1 else side_depth[side] == d
-            pl.when(has_side[side] & ready)(lambda: cross_own(side))
+            pl.when(has_side[side] & ready)(lambda: z_send(0, 1, z, side))
 
     expert = expert_ref[position]
     lane = lax.broadcasted_iota(jnp.int32, (1, 128), 1) - (128 - spare)
@@ -299,33 +296,28 @@
         up_pre[h] = lax.dot_general(xs[:replica, :], wu[h], contract, preferred_element_type=f32)
     sib_arrived(1, 0)
 
-    act_sends = [
-        pltpu.make_async_remote_copy(
-            src_ref=away_acts.at[k], dst_ref=acts.at[k, pl.ds(replica, replica)],
-            send_sem=act_send.at[k], recv_sem=act_recv.at[k], device_id=y_nbr, device_id_type=MESH,
-        )
-        for k in range(3)
-    ]
-    scale = jnp.sum(gs[:replica, tail:].astype(f32) * sel, axis=1, keepdims=True)
-    for h in (1, 0):
-        b = scale * lax.dot_general(
-            gs[:replica, :width], w[h, :, 2 * width :], contract, preferred_element_type=f32
-        )
+    def activate(h, ry, gate, up):
+        r = slice(ry * replica, (ry + 1) * replica)
+        scale = jnp.sum(gs[r, tail:].astype(f32) * sel, axis=1, keepdims=True)
+        b = scale * lax.dot_general(gs[r, :width], w[h, :, 2 * width :], contract, preferred_element_type=f32)
         unit = lax.broadcasted_iota(jnp.int32, (1, half), 1) + (y if h == 0 else 1 - y) * half
         unit_mask = jnp.where(unit < limit_ref[position], 1.0, 0.0)
-        g, v = gate_pre[h], up_pre[h]
+        g, v = gate[...], up[...]
         live = jnp.broadcast_to(unit_mask, g.shape) > 0.0
         sigma = 1.0 / (1.0 + jnp.exp(-g))
         active = g * sigma
         gg = jnp.where(live, b * v * (sigma * (1.0 + g * (1.0 - sigma))), 0.0).astype(bf16)
         gu = jnp.where(live, b * active, 0.0).astype(bf16)
-        hid = jnp.where(live, active * v * scale, 0.0).astype(bf16)
-        for k, value in enumerate((gg, gu, hid)):
-            if h == 0:
-                acts[k, :replica, :] = value
-            else:
-                away_acts[k] = value
-                act_sends[k].start()
+        if h == 0:
+            acts[0, r, :] = gg
+            acts[1, r, :] = gu
+            acts[2, r, :] = jnp.where(live, active * v * scale, 0.0).astype(bf16)
+        else:
+            away_acts[0] = gg
+            away_acts[1] = gu
+
+    for h in range(2):
+        activate(h, 0, gate_pre.at[h], up_pre.at[h])
 
     quarter = (width // 128 + STRIPS) // STRIPS * 128
     strips = [(at, min(at + quarter, width)) for at in range(0, width, quarter)]
@@ -399,31 +391,33 @@
         if i > 0:
             second_stage(i - 1)
     second_stage(count - 1)
-    for p in range(2):
-        for d in range(1, nz):
-            at_distance(d, functools.partial(cross_last, p))
+    for d in range(1, nz):
+        at_distance(d, cross_last)
+    for zz in range(nz):
+        arrived(0, 1, 1, zz)
+        sib_send(0, 1, 1, zz)
+    for rx in range(2):
         for zz in range(nz):
-            arrived(p, 1, 1, zz)
-            sib_send(p, 1, 1, zz)
-
-    def terms(k):
-        if k < 2:
-            if k == 0:
-                sib_arrived(0, 1)
-            act_sends[k].wait_recv()
-            weight_term(k, xs)
-        elif k == 2:
-            sib_arrived(1, 1)
-            act_sends[k].wait_recv()
-            weight_term(k, gs)
-
-    for i in range(count):
-        third_stage(i)
-        terms(i)
-    for k in range(count, 3):
-        terms(k)
-    store_w = pltpu.make_async_copy(gw, gw_out.at[0], local_sem.at[6])
-    store_w.start()
+            arrived(1, 1, rx, zz)
+            sib_send(1, 1, rx, zz)
+
+    def other_gate_up():
+        sib_arrived(0, 1)
+        r = slice(replica, 2 * replica)
+        gate_pre[0] = lax.dot_general(xs[r, :], w[0, :, :width], contract, preferred_element_type=f32)
+        up_pre[0] = lax.dot_general(xs[r, :], wu[0], contract, preferred_element_type=f32)
+
+    def other_acts():
+        sib_arrived(1, 1)
+        activate(0, 1, gate_pre.at[0], up_pre.at[0])
+        weight_term(0, xs)
+
+    fill = [other_gate_up, other_acts, functools.partial(weight_term, 1, xs), functools.partial(weight_term, 2, gs)]
+    for i in range(max(count, len(fill))):
+        if i < count:
+            third_stage(i)
+        if i < len(fill):
+            fill[i]()
 
     def sent(p, ry, side, chunks):
         s = slot(ry, 0, 0, 0)
@@ -431,17 +425,25 @@
 
     for p in range(2):
         for ry in range(2):
-            for side in range(2):
+            for side in range(2 if p == 0 or ry == 0 else 0):
                 for depth in range(nz - 1):
                     pl.when(side_depth[side] == depth)(lambda: sent(p, ry, side, depth + 1))
             move(p, 0, 0, sib, ss.at[p, ry], sib_recv.at[p, ry], 2 * nz).wait_send()
         move(p, 0, 0, x_nbr, sx.at[p], landing(p, 0, 1, 0), nz).wait_send()
-        move(p, 0, 0, y_nbr, sy.at[p], landing(p, 1, 0, 0), nz + 1).wait_send()
-    for copy in act_sends:
-        copy.wait_send()
+        move(p, 0, 0, y_nbr, sy.at[p], landing(p, 1, 0, 0), 2 * nz if p else nz + 1).wait_send()
     for i in range(count):
         last_stage(i)
-    store_w.wait()
+
+
+def store_kernel(gt, gw, gt_out, gw_out, sems):
+    copies = [
+        pltpu.make_async_copy(gt, gt_out, sems.at[0]),
+        pltpu.make_async_copy(gw, gw_out.at[0], sems.at[1]),
+    ]
+    for copy in copies:
+        copy.start()
+    for copy in copies:
+        copy.wait()
 
 
 def dense_shards(tokens, grad_out, route_ids, route_prob, device_expert, unit_count, expert_weights):
@@ -462,33 +464,42 @@
     any_spec = pl.BlockSpec(memory_space=pl.ANY)
     smem_spec = pl.BlockSpec(memory_space=pltpu.SMEM)
     vmem_spec = pl.BlockSpec(memory_space=pltpu.VMEM)
-    return pl.pallas_call(
+    kept = 2 * (tok * padded + half * (-(-3 * width // 128) * 128))
+    gt, gw = pl.pallas_call(
         functools.partial(split_kernel, nz, half, tok, width, experts),
-        out_shape=(
-            jax.ShapeDtypeStruct((tok, width), bf16),
-            jax.ShapeDtypeStruct((1, half, 3 * width), bf16),
-        ),
+        out_shape=(pltpu.VMEM((tok, width), bf16), pltpu.VMEM((half, 3 * width), bf16)),
         in_specs=[any_spec] * 5 + [smem_spec] * 2,
-        out_specs=(vmem_spec, any_spec),
+        out_specs=(vmem_spec, vmem_spec),
         scratch_shapes=[
             vmem((2 * replica, width), bf16), vmem((2 * replica, padded), bf16), vmem((tok, width), bf16),
             vmem((top, tok), jnp.int32), vmem((top, tok), f32),
             vmem((2, half, 3 * width), bf16), vmem((2, half, width), bf16),
             vmem((2, replica, half), f32), vmem((2, replica, half), f32),
-            vmem((3, 2 * replica, half), bf16), vmem((3, replica, half), bf16),
+            vmem((3, 2 * replica, half), bf16), vmem((2, replica, half), bf16),
             vmem((2 * line, width), f32),
             vmem((2 * line, width), bf16), vmem((2 * line, width), bf16),
             vmem((line, width), bf16), vmem((line, width), bf16),
             vmem((line, width), bf16), vmem(((nz - 1) * tok, width), bf16),
-            vmem((half, 3 * width), bf16),
-            dma((7,)), dma((2, 4 * nz)), dma((2, 2)), dma((8,)), dma((2,)), dma((2,)), dma((2, 2)),
-            dma((3,)), dma((3,)), dma((3 * STRIPS,)), dma((3 * STRIPS,)),
+            dma((6,)), dma((2, 4 * nz)), dma((2, 2)), dma((8,)), dma((2,)), dma((2,)), dma((2, 2)),
+            dma((3 * STRIPS,)), dma((3 * STRIPS,)),
         ],
         compiler_params=pltpu.CompilerParams(
-            collective_id=0, has_side_effects=True, vmem_limit_bytes=60 * 1024 * 1024
+            collective_id=0, has_side_effects=True, vmem_limit_bytes=VMEM_BYTES - kept
         ),
         name="split_backward",
     )(tokens, grad_out, expert_weights, route_ids.T, route_prob.T, device_expert, unit_count)
+    return pl.pallas_call(
+        store_kernel,
+        out_shape=(
+            jax.ShapeDtypeStruct((tok, width), bf16),
+            jax.ShapeDtypeStruct((1, half, 3 * width), bf16),
+        ),
+        in_specs=[vmem_spec] * 2,
+        out_specs=[any_spec] * 2,
+        scratch_shapes=[dma((2,))],
+        compiler_params=pltpu.CompilerParams(vmem_limit_bytes=1024 * 1024),
+        name="store_outputs",
+    )(gt, gw)
 
 
 def shards(tokens, grad_out, route_ids, *rest):

time: 53.4 us -> 47.9 us (0.90)
  local copies, waits for them, and re-layouts: 5.99 us -> 0 us
    unnamed x2 -> x0, local copies, waits for them, and re-layouts: 5.99 us -> none
    pallas_call x0 -> x1, Pallas kernels: none -> 2.05 us  [dense_shards(): pl.pallas_call(store_kernel, out_shape=(jax.ShapeDtypeStruct((tok, width)...]
    pallas_call x1, Pallas kernels: 46.6 us -> 45 us  [dense_shards(): pl.pallas_call(functools.partial(split_kernel, nz, half, tok, width, expe...]
where the time goes in v2:
time: 47.9 us; the launch traced here: 47.7 us
  Pallas kernels  47.1 us (98%)
  between operations  0.64 us (1%)
    pallas_call x1, Pallas kernels, dense_shards(): pl.pallas_call(functools.partial(split_kernel, nz, half, tok, width, expe...  45 us
    pallas_call x1, Pallas kernels, dense_shards(): pl.pallas_call(store_kernel, out_shape=(jax.ShapeDtypeStruct((tok, width)...  2.05 us

profile of v2, /device:TPU:0, one launch (start us, length us, event | category | flops | bytes accessed | tf_op | source)
XLA Modules:
  0.0 47.7 jit_solution(17443574563523481979)
XLA Ops:
  0.6 45.0 %split_backward.1 = (bf16[16,2880]{1,0:T(8,128)(2,1)S(1)}, bf16[240,8640]{1,0:T(8,128)(2,1)S(1)}) custom-call(bf16[16,2880]{1,0:T(8,128)(2,1)} %x_in.1, bf16[16,2880]{1,0:T(8,128)(2,1)} %g_in.1, bf16[1,480,8640]{2,1,0:T(8,128)(2,1)} %w_in.1, s32[4,16]{1,0:T(4,128)} %bitcast.2, f32[4,16]{1,0:T(4,128)} %bitcast.3, s32[16]{0:T(128)} %expert_ref.1, s32[16]{0:T(128)} %limit_ref.1), custom_call_target="tpu_custom_call" | custom-call | tf_op jit(solution)/shard_map/split_backward/pallas_call | solution.py:468
  45.6 2.1 %store_outputs.1 = (bf16[16,2880]{1,0:T(8,128)(2,1)}, bf16[1,240,8640]{2,1,0:T(8,128)(2,1)}) custom-call(bf16[16,2880]{1,0:T(8,128)(2,1)S(1)} %get-tuple-element.4.gt, bf16[240,8640]{1,0:T(8,128)(2,1)S(1)} %get-tuple-element.5.gw), custom_call_target="tpu_custom_call" | custom-call | tf_op jit(solution)/shard_map/store_outputs/pallas_call | solution.py:491

commit v3 on v2

--- a/solution.py
+++ b/solution.py
@@ -112,14 +112,15 @@
 
 MESH = pl.DeviceIdType.MESH
 STEP = 256
-STRIPS = 4
+STRIPS = 6
+FILLS = (1, 2, 3, 5, 6, 8)
 VMEM_BYTES = 67043328
 
 
 def split_kernel(
     nz, half, tok, width, experts,
     x_in, g_in, w_in, ids_in, prob_in, expert_ref, limit_ref, gt_out, gw,
-    xs, gs, own_g, ids, prob, w, wu, gate_pre, up_pre, acts, away_acts, acc,
+    xs, gs, own_g, ids, prob, w, wu, gate, up, slope, own_acts, acts, turned, acc,
     send1, recv1, send2, recv2, send3, recv3,
     local_sem, recv_sem, sib_recv, sz, sx, sy, ss, rs_send, rs_recv,
 ):
@@ -138,9 +139,12 @@
     has_side = (z > 0, z < nz - 1)
     side_depth = (nz - 1 - z, z)
     barrier = pltpu.get_barrier_semaphore()
-    peers = [x_nbr, y_nbr, sib] + z_nbrs
-    for peer in peers:
+    for peer in (x_nbr, y_nbr, sib):
         pl.semaphore_signal(barrier, inc=1, device_id=peer, device_id_type=MESH)
+    for side in range(2):
+        pl.when(has_side[side])(
+            lambda: pl.semaphore_signal(barrier, inc=1, device_id=z_sides[side], device_id_type=MESH)
+        )
 
     line = nz * tok
     side_rows = 2 * line
@@ -152,8 +156,8 @@
     def rows(s, count=1):
         return pl.ds(pl.multiple_of(s * tok, tok), count * tok)
 
-    mine = slot(0, 0, 0, z)
-    own_x = pltpu.make_async_copy(x_in, xs.at[rows(mine)], local_sem.at[0])
+    start = slot(0, 0, 0, z)
+    own_x = pltpu.make_async_copy(x_in, xs.at[rows(start)], local_sem.at[0])
     load_g = pltpu.make_async_copy(g_in, own_g, local_sem.at[1])
     load_ids = pltpu.make_async_copy(ids_in, ids, local_sem.at[2])
     load_prob = pltpu.make_async_copy(prob_in, prob, local_sem.at[3])
@@ -162,7 +166,7 @@
     load_w = []
     for h in range(2):
         first = pl.multiple_of((y if h == 0 else 1 - y) * half, 16)
-        load_w.append(pltpu.make_async_copy(w_in.at[0, pl.ds(first, half)], w.at[h], local_sem.at[4 + h]))
+        load_w.append(pltpu.make_async_copy(w_in.at[0, pl.ds(first, half)], w.at[pl.ds(h * half, half)], local_sem.at[4 + h]))
         load_w[h].start()
 
     spare = gs.shape[1] - width
@@ -184,10 +188,11 @@
     term = lane // experts
     packed = jnp.where(term == 0, high, jnp.where(term == 1, middle, scales - high - middle))
     load_g.wait()
-    gs[rows(mine), :width] = own_g[...]
-    gs[rows(mine), width:] = jnp.where(term < 3, packed, 0.0).astype(bf16)
+    gs[rows(start), :width] = own_g[...]
+    gs[rows(start), width:] = jnp.where(term < 3, packed, 0.0).astype(bf16)
     own_x.wait()
-    pl.semaphore_wait(barrier, len(peers))
+    at_end = (z == 0) | (z == nz - 1)
+    pl.semaphore_wait(barrier, jnp.where(at_end, 4, 5))
 
     bufs = (xs, gs)
 
@@ -225,19 +230,29 @@
         for side, zz in ((0, z - d), (1, z + d)):
             pl.when((zz >= 0) & (zz < nz))(functools.partial(act, side, zz))
 
-    def from_z(side, zz):
+    def from_z(d, side, zz):
         for p in range(2):
             arrived(p, 0, 0, zz)
             pl.when(has_side[1 - side])(lambda: z_send(p, 0, zz, 1 - side))
             x_send(p, zz)
-            if p == 1:
+            if p == 1 and d > 1:
                 y_send(1, 0, zz)
             sib_send(p, 0, 0, zz)
 
     def relay_x(p, zz):
         arrived(p, 0, 1, zz)
         sib_send(p, 0, 1, zz)
+
+    def relay_xy(p, zz):
+        relay_x(p, zz)
         y_send(p, 1, zz)
+
+    def x_cross(p):
+        move(p, slot(1, 0, 0, z), slot(1, 0, 1, z), x_nbr, sx.at[p], landing(p, 1, 1, z)).start()
+
+    def z_cross(side):
+        for p in range(2):
+            z_send(p, 1, z, side)
 
     def cross_relay(side, zz):
         def go():
@@ -260,18 +275,22 @@
         sib_send(p, 0, 0, z)
     late = nz - 2
     for d in range(1, nz):
-        at_distance(d, from_z)
+        at_distance(d, functools.partial(from_z, d))
         if d == 1:
             for p in range(2):
                 relay_x(p, z)
-            arrived(0, 1, 0, z)
-            sib_send(0, 1, 0, z)
+            for p in range(2):
+                arrived(p, 1, 0, z)
+                sib_send(p, 1, 0, z)
         elif d - 1 < late:
             for p in range(2):
-                at_distance(d - 1, lambda side, zz: relay_x(p, zz))
+                at_distance(d - 1, lambda side, zz: relay_xy(p, zz))
         for side in range(2):
             ready = side_depth[side] <= 1 if d == 1 else side_depth[side] == d
-            pl.when(has_side[side] & ready)(lambda: z_send(0, 1, z, side))
+            pl.when(has_side[side] & ready)(lambda: z_cross(side))
+
+    for p in range(2):
+        x_cross(p)
 
     expert = expert_ref[position]
     lane = lax.broadcasted_iota(jnp.int32, (1, 128), 1) - (128 - spare)
@@ -281,43 +300,41 @@
 
     for h in range(2):
         load_w[h].wait()
-        wu[h] = w[h, :, width : 2 * width]
+        wu[h * half : (h + 1) * half] = w[h * half : (h + 1) * half, width : 2 * width]
     at_distance(1, cross_relay)
     for d in range(late, nz):
-        at_distance(d, lambda side, zz: relay_x(0, zz))
+        at_distance(d, lambda side, zz: relay_xy(0, zz))
     sib_arrived(0, 0)
-    for h in range(2):
-        gate_pre[h] = lax.dot_general(xs[:replica, :], w[h, :, :width], contract, preferred_element_type=f32)
+    gate[...] = lax.dot_general(xs[:replica, :], w[:, :width], contract, preferred_element_type=f32)
     for d in range(late, nz):
-        at_distance(d, lambda side, zz: relay_x(1, zz))
+        at_distance(d, lambda side, zz: relay_xy(1, zz))
     for d in range(2, nz - 1):
         at_distance(d, cross_relay)
-    for h in range(2):
-        up_pre[h] = lax.dot_general(xs[:replica, :], wu[h], contract, preferred_element_type=f32)
+    up[...] = lax.dot_general(xs[:replica, :], wu[...], contract, preferred_element_type=f32)
+
+    def derive(units):
+        lane = lax.broadcasted_iota(jnp.int32, (1, units), 1)
+        unit = jnp.where(lane < half, lane + y * half, lane - y * half)
+        g = gate[:, :units]
+        live = jnp.broadcast_to(jnp.where(unit < limit_ref[position], 1.0, 0.0), g.shape) > 0.0
+        sigma = 1.0 / (1.0 + jnp.exp(-g))
+        gate[:, :units] = jnp.where(live, g * sigma, 0.0)
+        slope[:, :units] = jnp.where(live, up[:, :units] * (sigma * (1.0 + g * (1.0 - sigma))), 0.0)
+
+    def scale_of(r):
+        return jnp.sum(gs[r, tail:].astype(f32) * sel, axis=1, keepdims=True)
+
+    def back(r, units):
+        return scale_of(r) * lax.dot_general(
+            gs[r, :width], w[:units, 2 * width :], contract, preferred_element_type=f32
+        )
+
+    mine, other = slice(0, replica), slice(replica, 2 * replica)
+    derive(2 * half)
     sib_arrived(1, 0)
-
-    def activate(h, ry, gate, up):
-        r = slice(ry * replica, (ry + 1) * replica)
-        scale = jnp.sum(gs[r, tail:].astype(f32) * sel, axis=1, keepdims=True)
-        b = scale * lax.dot_general(gs[r, :width], w[h, :, 2 * width :], contract, preferred_element_type=f32)
-        unit = lax.broadcasted_iota(jnp.int32, (1, half), 1) + (y if h == 0 else 1 - y) * half
-        unit_mask = jnp.where(unit < limit_ref[position], 1.0, 0.0)
-        g, v = gate[...], up[...]
-        live = jnp.broadcast_to(unit_mask, g.shape) > 0.0
-        sigma = 1.0 / (1.0 + jnp.exp(-g))
-        active = g * sigma
-        gg = jnp.where(live, b * v * (sigma * (1.0 + g * (1.0 - sigma))), 0.0).astype(bf16)
-        gu = jnp.where(live, b * active, 0.0).astype(bf16)
-        if h == 0:
-            acts[0, r, :] = gg
-            acts[1, r, :] = gu
-            acts[2, r, :] = jnp.where(live, active * v * scale, 0.0).astype(bf16)
-        else:
-            away_acts[0] = gg
-            away_acts[1] = gu
-
-    for h in range(2):
-        activate(h, 0, gate_pre.at[h], up_pre.at[h])
+    b = back(mine, 2 * half)
+    own_acts[0] = (b * slope[...]).astype(bf16)
+    own_acts[1] = (b * gate[...]).astype(bf16)
 
     quarter = (width // 128 + STRIPS) // STRIPS * 128
     strips = [(at, min(at + quarter, width)) for at in range(0, width, quarter)]
@@ -346,10 +363,8 @@
     def first_stage(i):
         for at, size in spans(*strips[i]):
             span = slice(at, at + size)
-            value = jnp.dot(acts[0, :replica, :], w[0, :, span], preferred_element_type=f32)
-            value += jnp.dot(acts[1, :replica, :], wu[0, :, span], preferred_element_type=f32)
-            value += jnp.dot(away_acts[0], w[1, :, span], preferred_element_type=f32)
-            value += jnp.dot(away_acts[1], wu[1, :, span], preferred_element_type=f32)
+            value = jnp.dot(own_acts[0], w[:, span], preferred_element_type=f32)
+            value += jnp.dot(own_acts[1], wu[:, span], preferred_element_type=f32)
             send1[:, span] = value[side_rows:].astype(bf16)
             acc[:, span] = value[:side_rows]
         core[i].start()
@@ -380,57 +395,95 @@
             total = total + recv3[(k - 1) * tok : k * tok, span].astype(f32)
         gt_out[:, span] = total.astype(bf16)
 
-    def weight_term(k, right):
-        turned = acts[k].T
-        for at, size in spans(0, width):
-            value = jnp.dot(turned, right[:, at : at + size], preferred_element_type=f32)
+    cuts = spans(0, width)
+    middle = len(cuts) // 2
+
+    def weight_term(k, right, part):
+        if part == 0:
+            turned[...] = acts[k].T
+        for at, size in cuts[middle:] if part else cuts[:middle]:
+            value = jnp.dot(turned[...], right[:, at : at + size], preferred_element_type=f32)
             gw[:, k * width + at : k * width + at + size] = value.astype(bf16)
+
+    def keep_own():
+        for k in range(2):
+            acts[k, mine, :] = own_acts[k, :, :half]
+        acts[2, mine, :] = (gate[:, :half] * up[:, :half] * scale_of(mine)).astype(bf16)
+
+    def pass_rows():
+        for d in range(1, nz):
+            at_distance(d, cross_last)
+        for zz in range(nz):
+            arrived(0, 1, 1, zz)
+            sib_send(0, 1, 1, zz)
+
+    def pass_column(side, zz):
+        arrived(1, 1, 0, zz)
+        sib_send(1, 1, 0, zz)
+
+    def pass_grads():
+        for d in range(1, nz):
+            at_distance(d, pass_column)
+        for zz in range(nz):
+            arrived(1, 1, 1, zz)
+            sib_send(1, 1, 1, zz)
+
+    def other_gate():
+        sib_arrived(0, 1)
+        gate[:, :half] = lax.dot_general(xs[other, :], w[:half, :width], contract, preferred_element_type=f32)
+
+    def other_up():
+        up[:, :half] = lax.dot_general(xs[other, :], wu[:half], contract, preferred_element_type=f32)
+        derive(half)
+
+    def other_back():
+        sib_arrived(1, 1)
+        b = back(other, half)
+        acts[0, other, :] = (b * slope[:, :half]).astype(bf16)
+        acts[1, other, :] = (b * gate[:, :half]).astype(bf16)
+        acts[2, other, :] = (gate[:, :half] * up[:, :half] * scale_of(other)).astype(bf16)
+
+    fill = [pass_rows, pass_grads, keep_own, other_gate, other_up, other_back]
+    for k, right in enumerate((xs, xs, gs)):
+        for part in range(2):
+            fill.append(functools.partial(weight_term, k, right, part))
 
     for i in range(count):
         first_stage(i)
         if i > 0:
             second_stage(i - 1)
     second_stage(count - 1)
-    for d in range(1, nz):
-        at_distance(d, cross_last)
-    for zz in range(nz):
-        arrived(0, 1, 1, zz)
-        sib_send(0, 1, 1, zz)
-    for rx in range(2):
-        for zz in range(nz):
-            arrived(1, 1, rx, zz)
-            sib_send(1, 1, rx, zz)
-
-    def other_gate_up():
-        sib_arrived(0, 1)
-        r = slice(replica, 2 * replica)
-        gate_pre[0] = lax.dot_general(xs[r, :], w[0, :, :width], contract, preferred_element_type=f32)
-        up_pre[0] = lax.dot_general(xs[r, :], wu[0], contract, preferred_element_type=f32)
-
-    def other_acts():
-        sib_arrived(1, 1)
-        activate(0, 1, gate_pre.at[0], up_pre.at[0])
-        weight_term(0, xs)
-
-    fill = [other_gate_up, other_acts, functools.partial(weight_term, 1, xs), functools.partial(weight_term, 2, gs)]
-    for i in range(max(count, len(fill))):
-        if i < count:
+    done = 0
+    for i in range(-1, count):
+        if i >= 0:
             third_stage(i)
-        if i < len(fill):
-            fill[i]()
+        upto = FILLS[i + 1] if i + 1 < count else len(fill)
+        for act in fill[done:upto]:
+            act()
+        done = upto
 
     def sent(p, ry, side, chunks):
         s = slot(ry, 0, 0, 0)
         move(p, s, s, z_sides[side], sz.at[(p * 2 + ry) * 2 + side], landing(p, ry, 0, 0), chunks).wait_send()
 
+    def to_y(p, chunks):
+        move(p, 0, 0, y_nbr, sy.at[p], landing(p, 1, 0, 0), chunks).wait_send()
+
     for p in range(2):
         for ry in range(2):
-            for side in range(2 if p == 0 or ry == 0 else 0):
+            for side in range(2):
+                if p == 1 and ry == 1:
+                    pl.when(has_side[side])(lambda: sent(p, ry, side, 1))
+                    continue
                 for depth in range(nz - 1):
                     pl.when(side_depth[side] == depth)(lambda: sent(p, ry, side, depth + 1))
             move(p, 0, 0, sib, ss.at[p, ry], sib_recv.at[p, ry], 2 * nz).wait_send()
-        move(p, 0, 0, x_nbr, sx.at[p], landing(p, 0, 1, 0), nz).wait_send()
-        move(p, 0, 0, y_nbr, sy.at[p], landing(p, 1, 0, 0), 2 * nz if p else nz + 1).wait_send()
+        move(p, 0, 0, x_nbr, sx.at[p], landing(p, 0, 1, 0), nz + 1).wait_send()
+        if p == 0:
+            to_y(p, nz)
+        else:
+            pl.when(at_end)(lambda: to_y(p, 2 * nz - 2))
+            pl.when(jnp.logical_not(at_end))(lambda: to_y(p, 2 * nz - 3))
     for i in range(count):
         last_stage(i)
 
@@ -473,9 +526,9 @@
         scratch_shapes=[
             vmem((2 * replica, width), bf16), vmem((2 * replica, padded), bf16), vmem((tok, width), bf16),
             vmem((top, tok), jnp.int32), vmem((top, tok), f32),
-            vmem((2, half, 3 * width), bf16), vmem((2, half, width), bf16),
-            vmem((2, replica, half), f32), vmem((2, replica, half), f32),
-            vmem((3, 2 * replica, half), bf16), vmem((2, replica, half), bf16),
+            vmem((2 * half, 3 * width), bf16), vmem((2 * half, width), bf16),
+            vmem((replica, 2 * half), f32), vmem((replica, 2 * half), f32), vmem((replica, 2 * half), f32),
+            vmem((2, replica, 2 * half), bf16), vmem((3, 2 * replica, half), bf16), vmem((half, 2 * replica), bf16),
             vmem((2 * line, width), f32),
             vmem((2 * line, width), bf16), vmem((2 * line, width), bf16),
             vmem((line, width), bf16), vmem((line, width), bf16),

time: 47.9 us -> 46.1 us (0.962)
  Pallas kernels: 47.1 us -> 45.3 us
    pallas_call x1, Pallas kernels: 45 us -> 43.2 us  [dense_shards(): pl.pallas_call(functools.partial(split_kernel, nz, half, tok, width, expe...]
where the time goes in v3:
time: 46.1 us; the launch traced here: 45.9 us
  Pallas kernels  45.3 us (98%)
  between operations  0.64 us (1%)
    pallas_call x1, Pallas kernels, dense_shards(): pl.pallas_call(functools.partial(split_kernel, nz, half, tok, width, expe...  43.2 us
    pallas_call x1, Pallas kernels, dense_shards(): pl.pallas_call(store_kernel, out_shape=(jax.ShapeDtypeStruct((tok, width)...  2.05 us

profile of v3, /device:TPU:0, one launch (start us, length us, event | category | flops | bytes accessed | tf_op | source)
XLA Modules:
  0.0 45.9 jit_solution(8345828425274462690)
XLA Ops:
  0.6 43.2 %split_backward.1 = (bf16[16,2880]{1,0:T(8,128)(2,1)S(1)}, bf16[240,8640]{1,0:T(8,128)(2,1)S(1)}) custom-call(bf16[16,2880]{1,0:T(8,128)(2,1)} %x_in.1, bf16[16,2880]{1,0:T(8,128)(2,1)} %g_in.1, bf16[1,480,8640]{2,1,0:T(8,128)(2,1)} %w_in.1, s32[4,16]{1,0:T(4,128)} %bitcast.2, f32[4,16]{1,0:T(4,128)} %bitcast.3, s32[16]{0:T(128)} %expert_ref.1, s32[16]{0:T(128)} %limit_ref.1), custom_call_target="tpu_custom_call" | custom-call | tf_op jit(solution)/shard_map/split_backward/pallas_call | solution.py:521
  43.9 2.1 %store_outputs.1 = (bf16[16,2880]{1,0:T(8,128)(2,1)}, bf16[1,240,8640]{2,1,0:T(8,128)(2,1)}) custom-call(bf16[16,2880]{1,0:T(8,128)(2,1)S(1)} %get-tuple-element.4.gt, bf16[240,8640]{1,0:T(8,128)(2,1)S(1)} %get-tuple-element.5.gw), custom_call_target="tpu_custom_call" | custom-call | tf_op jit(solution)/shard_map/store_outputs/pallas_call | solution.py:544

commit v4 on v3

--- a/solution.py
+++ b/solution.py
@@ -119,8 +119,8 @@
 
 def split_kernel(
     nz, half, tok, width, experts,
-    x_in, g_in, w_in, ids_in, prob_in, expert_ref, limit_ref, gt_out, gw,
-    xs, gs, own_g, ids, prob, w, wu, gate, up, slope, own_acts, acts, turned, acc,
+    x_in, g_in, w_in, ids_in, prob_in, expert_in, limit_in, gt_out, gw,
+    xs, gs, own_g, ids, prob, expert_ref, limit_ref, w, wu, gate, up, slope, own_acts, acts, turned, acc,
     send1, recv1, send2, recv2, send3, recv3,
     local_sem, recv_sem, sib_recv, sz, sx, sy, ss, rs_send, rs_recv,
 ):
@@ -161,7 +161,9 @@
     load_g = pltpu.make_async_copy(g_in, own_g, local_sem.at[1])
     load_ids = pltpu.make_async_copy(ids_in, ids, local_sem.at[2])
     load_prob = pltpu.make_async_copy(prob_in, prob, local_sem.at[3])
-    for copy in (own_x, load_ids, load_prob, load_g):
+    load_expert = pltpu.make_async_copy(expert_in, expert_ref, local_sem.at[6])
+    load_limit = pltpu.make_async_copy(limit_in, limit_ref, local_sem.at[7])
+    for copy in (own_x, load_ids, load_prob, load_g, load_expert, load_limit):
         copy.start()
     load_w = []
     for h in range(2):
@@ -278,10 +280,13 @@
         at_distance(d, functools.partial(from_z, d))
         if d == 1:
             for p in range(2):
-                relay_x(p, z)
+                relay_xy(p, z)
             for p in range(2):
                 arrived(p, 1, 0, z)
                 sib_send(p, 1, 0, z)
+            for h in range(2):
+                load_w[h].wait()
+                wu[h * half : (h + 1) * half] = w[h * half : (h + 1) * half, width : 2 * width]
         elif d - 1 < late:
             for p in range(2):
                 at_distance(d - 1, lambda side, zz: relay_xy(p, zz))
@@ -289,18 +294,15 @@
             ready = side_depth[side] <= 1 if d == 1 else side_depth[side] == d
             pl.when(has_side[side] & ready)(lambda: z_cross(side))
 
-    for p in range(2):
-        x_cross(p)
-
+
+    load_expert.wait()
+    load_limit.wait()
     expert = expert_ref[position]
     lane = lax.broadcasted_iota(jnp.int32, (1, 128), 1) - (128 - spare)
     sel = jnp.where((lane >= 0) & (lane < 3 * experts) & (lane % experts == expert), 1.0, 0.0)
     contract = (((1,), (1,)), ((), ()))
     tail = width // 128 * 128
 
-    for h in range(2):
-        load_w[h].wait()
-        wu[h * half : (h + 1) * half] = w[h * half : (h + 1) * half, width : 2 * width]
     at_distance(1, cross_relay)
     for d in range(late, nz):
         at_distance(d, lambda side, zz: relay_xy(0, zz))
@@ -478,12 +480,12 @@
                 for depth in range(nz - 1):
                     pl.when(side_depth[side] == depth)(lambda: sent(p, ry, side, depth + 1))
             move(p, 0, 0, sib, ss.at[p, ry], sib_recv.at[p, ry], 2 * nz).wait_send()
-        move(p, 0, 0, x_nbr, sx.at[p], landing(p, 0, 1, 0), nz + 1).wait_send()
+        move(p, 0, 0, x_nbr, sx.at[p], landing(p, 0, 1, 0), nz).wait_send()
         if p == 0:
-            to_y(p, nz)
+            to_y(p, nz + 1)
         else:
-            pl.when(at_end)(lambda: to_y(p, 2 * nz - 2))
-            pl.when(jnp.logical_not(at_end))(lambda: to_y(p, 2 * nz - 3))
+            pl.when(at_end)(lambda: to_y(p, 2 * nz - 1))
+            pl.when(jnp.logical_not(at_end))(lambda: to_y(p, 2 * nz - 2))
     for i in range(count):
         last_stage(i)
 
@@ -515,17 +517,17 @@
     vmem = pltpu.VMEM
     dma = pltpu.SemaphoreType.DMA
     any_spec = pl.BlockSpec(memory_space=pl.ANY)
-    smem_spec = pl.BlockSpec(memory_space=pltpu.SMEM)
     vmem_spec = pl.BlockSpec(memory_space=pltpu.VMEM)
     kept = 2 * (tok * padded + half * (-(-3 * width // 128) * 128))
     gt, gw = pl.pallas_call(
         functools.partial(split_kernel, nz, half, tok, width, experts),
         out_shape=(pltpu.VMEM((tok, width), bf16), pltpu.VMEM((half, 3 * width), bf16)),
-        in_specs=[any_spec] * 5 + [smem_spec] * 2,
+        in_specs=[any_spec] * 7,
         out_specs=(vmem_spec, vmem_spec),
         scratch_shapes=[
             vmem((2 * replica, width), bf16), vmem((2 * replica, padded), bf16), vmem((tok, width), bf16),
             vmem((top, tok), jnp.int32), vmem((top, tok), f32),
+            pltpu.SMEM((devices,), jnp.int32), pltpu.SMEM((devices,), jnp.int32),
             vmem((2 * half, 3 * width), bf16), vmem((2 * half, width), bf16),
             vmem((replica, 2 * half), f32), vmem((replica, 2 * half), f32), vmem((replica, 2 * half), f32),
             vmem((2, replica, 2 * half), bf16), vmem((3, 2 * replica, half), bf16), vmem((half, 2 * replica), bf16),
@@ -533,7 +535,7 @@
             vmem((2 * line, width), bf16), vmem((2 * line, width), bf16),
             vmem((line, width), bf16), vmem((line, width), bf16),
             vmem((line, width), bf16), vmem(((nz - 1) * tok, width), bf16),
-            dma((6,)), dma((2, 4 * nz)), dma((2, 2)), dma((8,)), dma((2,)), dma((2,)), dma((2, 2)),
+            dma((8,)), dma((2, 4 * nz)), dma((2, 2)), dma((8,)), dma((2,)), dma((2,)), dma((2, 2)),
             dma((3 * STRIPS,)), dma((3 * STRIPS,)),
         ],
         compiler_params=pltpu.CompilerParams(

time: 46.1 us -> 45.3 us (0.983)
  Pallas kernels: 45.3 us -> 44.5 us
    pallas_call x1, Pallas kernels: 43.2 us -> 42.4 us  [dense_shards(): pl.pallas_call(functools.partial(split_kernel, nz, half, tok, width, expe...]
where the time goes in v4:
time: 45.3 us; the launch traced here: 45.1 us
  Pallas kernels  44.5 us (98%)
  between operations  0.64 us (1%)
    pallas_call x1, Pallas kernels, dense_shards(): pl.pallas_call(functools.partial(split_kernel, nz, half, tok, width, expe...  42.4 us
    pallas_call x1, Pallas kernels, dense_shards(): pl.pallas_call(store_kernel, out_shape=(jax.ShapeDtypeStruct((tok, width)...  2.05 us

profile of v4, /device:TPU:0, one launch (start us, length us, event | category | flops | bytes accessed | tf_op | source)
XLA Modules:
  0.0 45.1 jit_solution(7577742248413335264)
XLA Ops:
  0.6 42.4 %split_backward.1 = (bf16[16,2880]{1,0:T(8,128)(2,1)S(1)}, bf16[240,8640]{1,0:T(8,128)(2,1)S(1)}) custom-call(bf16[16,2880]{1,0:T(8,128)(2,1)} %x_in.1, bf16[16,2880]{1,0:T(8,128)(2,1)} %g_in.1, bf16[1,480,8640]{2,1,0:T(8,128)(2,1)} %w_in.1, s32[4,16]{1,0:T(4,128)} %bitcast.2, f32[4,16]{1,0:T(4,128)} %bitcast.3, s32[16]{0:T(128)} %expert_in.1, s32[16]{0:T(128)} %limit_in.1), custom_call_target="tpu_custom_call" | custom-call | tf_op jit(solution)/shard_map/split_backward/pallas_call | solution.py:522
  43.1 2.1 %store_outputs.1 = (bf16[16,2880]{1,0:T(8,128)(2,1)}, bf16[1,240,8640]{2,1,0:T(8,128)(2,1)}) custom-call(bf16[16,2880]{1,0:T(8,128)(2,1)S(1)} %get-tuple-element.4.gt, bf16[240,8640]{1,0:T(8,128)(2,1)S(1)} %get-tuple-element.5.gw), custom_call_target="tpu_custom_call" | custom-call | tf_op jit(solution)/shard_map/store_outputs/pallas_call | solution.py:546
